TPU v7x, 512 devices: a whole 4x8x8 slice. The times are simulated.
512 devices in a mesh: row: 32 (over z_hi, y, core), col: 16 (over z_lo, x).
Axes of the slice: x: 4, y: 8, z: 8 (z_hi: 2, z_lo: 4; z = z_hi * 4 + z_lo), core: 2. Of those that a mesh axis runs over, the one named last changes fastest.
Arguments:
- features: float32 [24576, 256], P(('row', 'col')), may hold values from -6 to 6
- inv_scale: float32 [256], replicated, may hold values from 0.001953125 to 0.015625
- probe_u: float32 [24576, 64], P(('row', 'col')), may hold values from -6 to 6
- solve_v: float32 [24576, 64], P(('row', 'col')), may hold values from -6 to 6
Outputs:
- feature_grad: float32 [24576, 256], P(('row', 'col'))
All inputs are finite; a program needn't handle non-finite values.
Results may differ from a plain program's by a relative error of at most 0.0003.
Values sent between devices are 32-bit elements; how exact they have to be, the bound alone decides.
No kernel may reach another device: no remote copies, remote signals or barrier semaphores. Data moves between devices by JAX's collectives and lax.ppermute only.
A program may use at most 64 MiB of HBM per device.

v0:
```python
import jax
import jax.numpy as jnp
from jax import lax
from jax.sharding import PartitionSpec as P


def tile_terms(row_x, row_left, col_x, col_right, inv_scale):
    col_scaled = col_x * inv_scale
    row_sq = jnp.sum(row_x * inv_scale * row_x, axis=1)
    col_sq = jnp.sum(col_scaled * col_x, axis=1)
    contract_last = (((1,), (1,)), ((), ()))
    inner_prod = lax.dot_general(
        row_x,
        col_scaled,
        contract_last,
        precision=lax.Precision.HIGHEST,
        preferred_element_type=jnp.float32,
    )
    mixing = lax.dot_general(
        row_left,
        col_right,
        contract_last,
        precision=lax.Precision.HIGHEST,
        preferred_element_type=jnp.float32,
    )
    coupling = mixing * jnp.exp(-0.5 * (row_sq[:, None] + col_sq[None, :] - 2.0 * inner_prod))
    row_pull = jnp.dot(
        coupling, col_x, precision=lax.Precision.HIGHEST, preferred_element_type=jnp.float32
    )
    col_pull = lax.dot_general(
        coupling,
        row_x,
        (((0,), (0,)), ((), ())),
        precision=lax.Precision.HIGHEST,
        preferred_element_type=jnp.float32,
    )
    row_term = (row_pull - jnp.sum(coupling, axis=1)[:, None] * row_x) * inv_scale
    col_term = (col_pull - jnp.sum(coupling, axis=0)[:, None] * col_x) * inv_scale
    return (row_term, col_term)


def on_device(features, inv_scale, probe_u, solve_v):
    local_rows = features.shape[0]
    row_x, row_u = (
        lax.all_gather(features, "col", axis=0, tiled=True),
        lax.all_gather(probe_u, "col", axis=0, tiled=True),
    )
    col_x, col_v = (
        lax.all_gather(features, "row", axis=0, tiled=True),
        lax.all_gather(solve_v, "row", axis=0, tiled=True),
    )
    row_acc, col_acc = tile_terms(row_x, row_u, col_x, col_v, inv_scale)
    row_whole = lax.psum(row_acc, "col")
    col_whole = lax.psum(col_acc, "row")
    row_own = lax.dynamic_slice_in_dim(row_whole, lax.axis_index("col") * local_rows, local_rows, 0)
    col_own = lax.dynamic_slice_in_dim(col_whole, lax.axis_index("row") * local_rows, local_rows, 0)
    return row_own + col_own


def solution(mesh):
    return jax.shard_map(
        on_device,
        mesh=mesh,
        in_specs=(P(("row", "col"), None), P(), P(("row", "col"), None), P(("row", "col"), None)),
        out_specs=P(("row", "col"), None),
        check_vma=False,
    )
```

profile of v0, /device:TPU:1, one launch (start us, length us, event | category | flops | bytes accessed | tf_op | source)
XLA Modules:
  0.0 697.5 jit_solution(9515123725436613279)
XLA Ops:
  6.5 0.0 copy-start.3
  6.5 0.0 all-gather.2.cloned.1.call-start
  6.5 0.7 all-gather.2.cloned.1.call-update
  7.3 0.0 all-reduce.3.cloned.1.call-start
  7.3 41.2 %all_gather.12 = f32[768,64]{1,0:T(8,128)S(1)} all-gather(f32[48,64]{1,0:T(8,128)} %param.6), channel_id=1, replica_groups=mesh['row'=32,'col'=16] {'col'}, dimensions={0}, use_global_device_ids=true | all-gather | bytes 208896 | tf_op jit(solution)/shard_map/all_gather | solution.py:46
  48.5 37.8 %all_gather.14 = f32[768,256]{1,0:T(8,128)S(1)} all-gather(f32[48,256]{1,0:T(8,128)} %param.4), channel_id=1, replica_groups=mesh['row'=32,'col'=16] {'col'}, dimensions={0}, use_global_device_ids=true | all-gather | bytes 835584 | tf_op jit(solution)/shard_map/all_gather | solution.py:45
  86.3 0.9 fusion.7
  87.2 0.0 copy-done.3
  87.2 71.8 %all_gather.13 = f32[1536,64]{1,0:T(8,128)S(1)} all-gather(f32[48,64]{1,0:T(8,128)S(1)} %copy-done.3), channel_id=1, replica_groups=mesh['row'=32,'col'=16] {'row'}, dimensions={0}, use_global_device_ids=true | all-gather | bytes 405504 | tf_op jit(solution)/shard_map/all_gather | solution.py:50
  159.0 0.0 copy-start.2
  159.0 5.5 fusion.10
  164.5 0.0 all-gather.2.cloned.1.call-done
  164.5 0.0 copy-done.2
  164.5 0.0 copy-start.1
  164.5 1.8 fusion.5
  166.3 0.1 copy-done.1
  166.4 7.4 %fusion.9 = (f32[768]{0:T(1024)S(1)}, f32[1536]{0:T(1024)S(1)}, f32[768,1536]{1,0:T(8,128)S(1)}) fusion(f32[768,1536]{1,0:T(8,128)} %fusion.10, f32[768,256]{1,0:T(8,128)S(1)} %all_gather.14, f32[1536,256]{1,0:T(8,128)S(1)} %copy-done.1, f32[256]{0:T(256)S(1)} %copy-done.2, f32[1536]{0:T(1024)S(1)} %fusion.5, f32[768]{0:T(1024)S(1)} %fusion.7), kind=kOutput, calls=%fused_computation.15 | convolution fusion | flops 3632527104 | bytes 11815936 | tf_op jit(solution)/shard_map/dot_general | solution.py:12
  173.8 0.0 copy-start
  173.8 2.1 copy-done
  175.9 4.7 fusion.6
  180.6 0.0 all-reduce.3.cloned.1.call-update
  180.7 0.2 all-reduce.5.cloned.1.call-start
  180.9 11.2 %fusion.3 = f32[1536,256]{1,0:T(8,128)} fusion(f32[768,1536]{1,0:T(8,128)} %copy-done, f32[768,256]{1,0:T(8,128)S(1)} %all_gather.14, f32[1536,256]{1,0:T(8,128)S(1)} %copy-done.1, f32[1536]{0:T(1024)S(1)} %get-tuple-element.6, f32[256]{0:T(256)S(1)} %copy-done.2), kind=kOutput, calls=%fused_computation.5 | convolution fusion | flops 3625058304 | bytes 8657920 | tf_op jit(solution)/shard_map/dot_general | solution.py:30
  192.1 0.0 all-reduce.5.cloned.1.call-update
  192.2 137.3 %all-reduce.3.cloned.1.call-done = f32[768,256]{1,0:T(8,128)} async-done(((f32[768,256]{1,0:T(8,128)}), f32[768,256]{1,0:T(8,128)}) %all-reduce.3.cloned.1.call-update) | async-done | bytes 786448 | tf_op jit(solution)/shard_map/psum | solution.py:53
  329.4 360.1 %all-reduce.5.cloned.1.call-done = f32[1536,256]{1,0:T(8,128)} async-done(((f32[1536,256]{1,0:T(8,128)}), f32[1536,256]{1,0:T(8,128)}) %all-reduce.5.cloned.1.call-update) | async-done | bytes 1572880 | tf_op jit(solution)/shard_map/psum | solution.py:54
  689.5 1.4 dynamic-slice_add_fusion
Async XLA Ops:
  6.5 80.6 %copy-start.3 = (f32[48,64]{1,0:T(8,128)S(1)}, f32[48,64]{1,0:T(8,128)}, u32[]{:S(2)}) copy-start(f32[48,64]{1,0:T(8,128)} %param.7) | copy-start | bytes 36868
  6.5 157.9 %all-gather.2.cloned.1.call-start = ((), (), s32[]{:S(2)}) async-start(), calls=%async_computation | async-start | bytes 1622016 | tf_op jit(solution)/shard_map/all_gather | solution.py:49
  7.3 322.2 %all-reduce.3.cloned.1.call-start = ((), (), s32[]{:S(2)}) async-start(), calls=%async_computation.1 | async-start | bytes 1572864 | tf_op jit(solution)/shard_map/psum | solution.py:53
  159.0 5.5 copy-start.2
  164.5 1.9 copy-start.1
  173.8 2.1 copy-start
  180.7 508.9 %all-reduce.5.cloned.1.call-start = ((), (), s32[]{:S(2)}) async-start(), calls=%async_computation.2 | async-start | bytes 3145728 | tf_op jit(solution)/shard_map/psum | solution.py:54
Sparse Core Ops, SparseCore 0:
  10.7 93.6 all-gather.1
  180.8 148.6 all-reduce.2
  332.4 357.1 all-reduce.4
where the time goes:
time: 698 us
  waiting for transfers between devices  498 us (71%)
  blocking collectives  151 us (22%)
  matrix products  28.9 us (4%)
  between operations  13.2 us (2%)
    psum x1, waiting for transfers between devices, on_device(): col_whole = lax.psum(col_acc, 'row')  360 us
    psum x1, waiting for transfers between devices, on_device(): row_whole = lax.psum(row_acc, 'col')  137 us
    all_gather x1, blocking collectives, on_device(): lax.all_gather(solve_v, 'row', axis=0, tiled=True)  71.8 us
    all_gather x1, blocking collectives, on_device(): lax.all_gather(probe_u, 'col', axis=0, tiled=True)  41.2 us
    all_gather x1, blocking collectives, on_device(): lax.all_gather(features, 'col', axis=0, tiled=True)  37.8 us
  transfers between devices with their start and end apart: 3, of which 2 were waited for; matrix products, arithmetic and copies ran while one was open for 3% of the time, Pallas kernels for 0%

commit v1 on v0

v1 whole, which is shorter than its diff:
```python
import functools

import jax
import jax.numpy as jnp
from jax import lax
from jax.experimental import pallas as pl
from jax.experimental.pallas import tpu as pltpu
from jax.sharding import Mesh, PartitionSpec as P

NT = (((1,), (1,)), ((), ()))
NN = (((1,), (0,)), ((), ()))

AXES = ("zh", "yh", "yl", "core", "zm", "zb", "x")
SIZES = (2, 4, 2, 2, 2, 2, 4)
BRICK = ("yl", "zb", "x")
FAR = ("yh", "zh", "zm")


def split(a):
    hi = a.astype(jnp.bfloat16)
    return hi, (a - hi.astype(jnp.float32)).astype(jnp.bfloat16)


def dot(a, b, dims):
    return lax.dot_general(a, b, dims, preferred_element_type=jnp.float32)


def tile_kernel(first, last, inv_ref, row_ref, col_ref, *refs):
    if first:
        out_ref, sum_ref, row_x3, row_w3, row_q, row_sum = refs
    else:
        acc_ref, acc_sum_ref, out_ref, row_x3, row_w3, row_q, row_sum = refs
    step = pl.program_id(0)
    width = inv_ref.shape[1]
    rank = (row_ref.shape[1] - width) // 2
    inv = inv_ref[...]

    @pl.when(step == 0)
    def _():
        x = row_ref[:, :width]
        scaled = x * inv
        hi, lo = split(scaled)
        row_x3[...] = jnp.concatenate([hi, lo, hi], axis=1)
        row_q[...] = jnp.broadcast_to(
            -0.5 * jnp.sum(scaled * x, axis=1, keepdims=True), row_q.shape
        )
        hi, lo = split(pltpu.roll(row_ref[:, width:], rank, 1))
        row_w3[...] = jnp.concatenate([hi, lo, hi], axis=1)
        if first:
            out_ref[...] = jnp.zeros_like(out_ref)
            row_sum[...] = jnp.zeros_like(row_sum)
        else:
            out_ref[...] = acc_ref[...]
            row_sum[...] = acc_sum_ref[...]

    col_x = col_ref[:, :width]
    x_hi, x_lo = split(col_x)
    w_hi, w_lo = split(col_ref[:, width:])
    col_q = lax.dot_general(
        jnp.full((8, width), -0.5, jnp.float32),
        col_x * col_x * inv,
        NT,
        precision=lax.Precision.HIGHEST,
        preferred_element_type=jnp.float32,
    )[:1]
    inner = dot(row_x3[...], jnp.concatenate([x_hi, x_hi, x_lo], axis=1), NT)
    mixing = dot(row_w3[...], jnp.concatenate([w_hi, w_hi, w_lo], axis=1), NT)
    lanes = row_q.shape[1]
    parts = col_x.shape[0] // lanes
    q = jnp.concatenate([row_q[...]] * parts, axis=1) + col_q
    coupling = mixing * jnp.exp(inner + q)
    c_hi, c_lo = split(coupling)
    sums = row_sum[...]
    for part in range(parts):
        sums = sums + coupling[:, part * lanes : (part + 1) * lanes]
    row_sum[...] = sums
    out_ref[...] += dot(
        jnp.concatenate([c_hi, c_lo, c_hi], axis=1),
        jnp.concatenate([x_hi, x_hi, x_lo], axis=0),
        NN,
    )

    @pl.when(step == pl.num_programs(0) - 1)
    def _():
        if last:
            total = jnp.sum(row_sum[...], axis=1, keepdims=True)
            out_ref[...] = (out_ref[...] - total * row_ref[:, :width]) * inv
        else:
            sum_ref[...] = row_sum[...]


def tile_terms(inv_scale, rows, cols, chunk, before=None):
    width = inv_scale.shape[0]
    n_rows, packed = rows.shape
    rank2 = packed - width
    first = before is None
    whole = lambda lanes: pl.BlockSpec((n_rows, lanes), lambda j: (0, 0))
    shape = lambda lanes: jax.ShapeDtypeStruct((n_rows, lanes), jnp.float32)
    specs = [
        pl.BlockSpec((1, width), lambda j: (0, 0)),
        whole(packed),
        pl.BlockSpec((chunk, packed), lambda j: (j, 0)),
    ]
    return pl.pallas_call(
        functools.partial(tile_kernel, first, not first),
        grid=(cols.shape[0] // chunk,),
        in_specs=specs if first else [*specs, whole(width), whole(128)],
        out_specs=[whole(width), whole(128)] if first else whole(width),
        out_shape=[shape(width), shape(128)] if first else shape(width),
        scratch_shapes=[
            pltpu.VMEM((n_rows, 3 * width), jnp.bfloat16),
            pltpu.VMEM((n_rows, 3 * rank2), jnp.bfloat16),
            pltpu.VMEM((n_rows, 128), jnp.float32),
            pltpu.VMEM((n_rows, 128), jnp.float32),
        ],
    )(inv_scale.reshape(1, width), rows, cols, *(before or ()))


def spread(block, axes, count):
    copies = jnp.broadcast_to(block[None], (count, *block.shape))
    return lax.all_to_all(copies, axes, 0, 0, tiled=True)


def on_device(features, inv_scale, probe_u, solve_v):
    local, width = features.shape
    own = jnp.concatenate([features, probe_u, solve_v], axis=1)
    cols = spread(own, FAR, 16).reshape(16 * local, -1)
    other = lax.ppermute(cols, "core", [(0, 1), (1, 0)])
    rows = spread(own, BRICK, 16).reshape(16 * local, -1)
    begun = tile_terms(inv_scale, rows, cols, 384)
    terms = tile_terms(inv_scale, rows, other, 384, begun)
    shares = lax.all_to_all(terms.reshape(16, local, width), BRICK, 0, 0, tiled=True)
    return jnp.sum(shares, axis=0)


def solution(mesh):
    parts = Mesh(mesh.devices.reshape(SIZES), AXES)
    return jax.shard_map(
        on_device,
        mesh=parts,
        in_specs=(P(AXES, None), P(), P(AXES, None), P(AXES, None)),
        out_specs=P(AXES, None),
        check_vma=False,
    )
```

time: 698 us -> 115 us (0.16)
  waiting for transfers between devices: 498 us -> 12.5 us
  blocking collectives: 151 us -> 70.3 us
  matrix products: 28.9 us -> 0 us
  Pallas kernels: 0 us -> 17 us
  between operations: 13.2 us -> 0.03 us
  starting transfers between devices: 0.26 us -> 8.2 us
    psum x2 -> x0, waiting for transfers between devices: 497 us -> none  [the longest x1 360 us: on_device(): col_whole = lax.psum(col_acc, 'row')]
    all_gather x3 -> x0, blocking collectives: 151 us -> none  [the longest x1 71.8 us: on_device(): lax.all_gather(solve_v, 'row', axis=0, tiled=True)]
    all_to_all x0 -> x2, blocking collectives: none -> 70.3 us  [the longest x1 55.4 us: spread(): return lax.all_to_all(copies, axes, 0, 0, tiled=True)]
    dot_general x4 -> x0, matrix products: 28.9 us -> none  [the longest x1 11.2 us: tile_terms(): lax.dot_general(coupling, row_x, (((0,), (0,)), ((), ())), precision=lax....]
    pallas_call x0 -> x2, Pallas kernels: none -> 17 us  [tile_terms(): pl.pallas_call(functools.partial(tile_kernel, first, not first), grid=(co...]
    all_to_all x0 -> x1, waiting for transfers between devices: none -> 12.5 us  [spread(): return lax.all_to_all(copies, axes, 0, 0, tiled=True)]
  transfers between devices with their start and end apart: 3 -> 2, of which waited for: 2 -> 1; matrix products, arithmetic and copies ran while one was open for 3% -> 0% of each run, Pallas kernels for 0% -> 7%
where the time goes in v1:
time: 115 us; the launch traced here: 113 us
  blocking collectives  70.3 us (61%)
  Pallas kernels  17 us (15%)
  waiting for transfers between devices  12.5 us (11%)
  starting transfers between devices  8.2 us (7%)
  local copies, waits for them, and re-layouts  3.15 us (3%)
  other arithmetic  1.58 us (1%)
    all_to_all x1, blocking collectives, spread(): return lax.all_to_all(copies, axes, 0, 0, tiled=True)  55.4 us
    pallas_call x2, Pallas kernels, tile_terms(): pl.pallas_call(functools.partial(tile_kernel, first, not first), grid=(co...  17 us
    all_to_all x1, blocking collectives, on_device(): lax.all_to_all(terms.reshape(16, local, width), BRICK, 0, 0, tiled=True)  14.9 us
    all_to_all x1, waiting for transfers between devices, spread(): return lax.all_to_all(copies, axes, 0, 0, tiled=True)  12.5 us
    all_to_all x1, starting transfers between devices, spread(): return lax.all_to_all(copies, axes, 0, 0, tiled=True)  4.12 us
    ppermute x1, starting transfers between devices, on_device(): other = lax.ppermute(cols, 'core', [(0, 1), (1, 0)])  4.08 us
  transfers between devices with their start and end apart: 2, of which 1 were waited for; matrix products, arithmetic and copies ran while one was open for 0% of the time, Pallas kernels for 7%

profile of v1, /device:TPU:1, one launch (start us, length us, event | category | flops | bytes accessed | tf_op | source)
XLA Modules:
  0.0 112.8 jit_solution(12395038642121897253)
XLA Ops:
  0.0 0.9 pad_maximum_fusion
  0.9 1.1 broadcast_in_dim.2
  2.0 55.4 %all_to_all.15 = f32[16,48,384]{2,1,0:T(8,128)S(1)} all-to-all(f32[16,48,384]{2,1,0:T(8,128)} %broadcast_in_dim.2), channel_id=1, replica_groups=mesh['zh'=2,'yh'=4,'yl'=2,'core'=2,'zm'=2,'zb'=2,'x'=4] {'yh','zh','zm'}, dimensions={0} | all-to-all | bytes 2359296 | tf_op jit(solution)/shard_map/all_to_all | solution.py:121
  57.4 0.0 copy-start.1
  57.4 4.1 %all-to-all-start = ((f32[16,48,384]{2,1,0:T(8,128)}), f32[16,48,384]{2,1,0:T(8,128)S(1)}, u32[]{:S(2)}, u32[]{:S(2)}) async-start(f32[16,48,384]{2,1,0:T(8,128)} %broadcast_in_dim.2), calls=%async_computation | async-start | bytes 2359296 | tf_op jit(solution)/shard_map/all_to_all | solution.py:121
  61.5 0.0 copy-done.1
  61.5 4.1 %collective-permute-start = (f32[768,384]{1,0:T(8,128)S(1)}, f32[768,384]{1,0:T(8,128)S(1)}, u32[]{:S(2)}, u32[]{:S(2)}) collective-permute-start(f32[768,384]{1,0:T(8,128)S(1)} %bitcast.6), channel_id=1, source_target_pairs={{0,16},{16,0},{1,17},{17,1},{2,18},{18,2},{3,19},{19,3},{4,20},{20... | collective-permute-start | bytes 3538952 | tf_op jit(solution)/shard_map/ppermute | solution.py:128
  65.6 12.5 %all-to-all-done = f32[16,48,384]{2,1,0:T(8,128)S(1)} async-done(((f32[16,48,384]{2,1,0:T(8,128)}), f32[16,48,384]{2,1,0:T(8,128)S(1)}, u32[]{:S(2)}, u32[]{:S(2)}) %all-to-all-start) | async-done | bytes 1179680 | tf_op jit(solution)/shard_map/all_to_all | solution.py:121
  78.1 0.0 copy-start
  78.1 1.0 copy-done
  79.2 8.3 %shard_map.46 = (f32[768,256]{1,0:T(8,128)}, f32[768,128]{1,0:T(8,128)}) custom-call(f32[1,256]{1,0:T(1,128)} %bitcast.9, f32[768,384]{1,0:T(8,128)} %bitcast.4, f32[768,384]{1,0:T(8,128)} %bitcast.7), custom_call_target="tpu_custom_call" | custom-call | tf_op jit(solution)/shard_map/pallas_call | solution.py:104
  87.5 0.0 collective-permute-done.col_ref
  87.5 0.0 copy-start.2
  87.5 1.0 copy-done.2
  88.5 8.6 %shard_map.47 = f32[768,256]{1,0:T(8,128)} custom-call(f32[1,256]{1,0:T(1,128)} %bitcast.10, f32[768,384]{1,0:T(8,128)} %bitcast.5, f32[768,384]{1,0:T(8,128)} %copy-done.2, f32[768,256]{1,0:T(8,128)} %get-tuple-element.7.refs_0_, f32[768,128]{1,0:T(8,128)} %get-tuple-element.8.refs_1_), custom_call_target="tpu_custom_call" | custom-call | tf_op jit(solution)/shard_map/pallas_call | solution.py:104
  97.2 14.9 %all_to_all.16 = f32[16,48,256]{2,1,0:T(8,128)S(1)} all-to-all(f32[16,48,256]{2,1,0:T(8,128)} %bitcast.8), channel_id=1, replica_groups=mesh['zh'=2,'yh'=4,'yl'=2,'core'=2,'zm'=2,'zb'=2,'x'=4] {'yl','zb','x'}, dimensions={0} | all-to-all | bytes 1572864 | tf_op jit(solution)/shard_map/all_to_all | solution.py:132
  112.1 0.7 reduce_sum.9
Async XLA Ops:
  57.4 4.1 %copy-start.1 = (f32[16,48,384]{2,1,0:T(8,128)}, f32[16,48,384]{2,1,0:T(8,128)S(1)}, u32[]{:S(2)}) copy-start(f32[16,48,384]{2,1,0:T(8,128)S(1)} %all_to_all.15) | copy-start | bytes 3538948
  57.4 20.8 %all-to-all-start = ((f32[16,48,384]{2,1,0:T(8,128)}), f32[16,48,384]{2,1,0:T(8,128)S(1)}, u32[]{:S(2)}, u32[]{:S(2)}) async-start(f32[16,48,384]{2,1,0:T(8,128)} %broadcast_in_dim.2), calls=%async_computation | async-start | bytes 2359296 | tf_op jit(solution)/shard_map/all_to_all | solution.py:121
  61.5 26.0 %collective-permute-start = (f32[768,384]{1,0:T(8,128)S(1)}, f32[768,384]{1,0:T(8,128)S(1)}, u32[]{:S(2)}, u32[]{:S(2)}) collective-permute-start(f32[768,384]{1,0:T(8,128)S(1)} %bitcast.6), channel_id=1, source_target_pairs={{0,16},{16,0},{1,17},{17,1},{2,18},{18,2},{3,19},{19,3},{4,20},{20... | collective-permute-start | bytes 3538952 | tf_op jit(solution)/shard_map/ppermute | solution.py:128
  78.1 1.0 copy-start
  87.5 1.0 copy-start.2
